TPU v7x, 32 devices: a whole 2x2x4 slice. The times are simulated.
32 devices in a mesh: gx: 4 (over y, x), gy: 4 (over z), gz: 2 (over core).
Axes of the slice: x: 2, y: 2, z: 4, core: 2. Of those that a mesh axis runs over, the one named last changes fastest.
Arguments:
- functions: bfloat16 [2560, 8, 4096], P(('gx', 'gy', 'gz')), may hold values from -6 to 6
- responses: bfloat16 [2560, 8, 4096], P(('gx', 'gy', 'gz')), may hold values from -6 to 6
- box_domain: int32 [2560, 1], P(('gx', 'gy', 'gz')), may hold values from 0 to 31, as said below
- pair_index: int32 [2, 2560, 24], P(None, ('gx', 'gy', 'gz')), may hold values from 0 to 7
- pair_weight: float32 [2560, 24], P(('gx', 'gy', 'gz')), may hold values from -6 to 6
- kernel_xc: float32 [32, 8192], P(('gx', 'gy', 'gz')), may hold values from 0.25 to 2
Outputs:
- applied: bfloat16 [2560, 8, 4096], P(('gx', 'gy', 'gz'))
- potential: bfloat16 [32, 8192], P(('gx', 'gy', 'gz'))
Inputs may be any that keep to these rules, and one draw needn't show every extreme that they name: `box_domain`: boxes are held near their grid in y and z: a box of the device with mesh coordinates (ix, iy, iz) names domain ((ix + dx) mod 4, (iy + dy) mod 4, (iz + dz) mod 2) with dx in -2, -1, 0, dy in -1, 0 and dz in -1, 0, 1, and every device's boxes use all eighteen such offsets.
All inputs are finite; a program needn't handle non-finite values.
Results may differ from a plain program's by a relative error of at most 0.017.
Values may be sent and summed in bfloat16 or wider, within the bound.
A program may use at most 128 MiB of HBM per device.

v0:
```python
import math

import jax
import jax.numpy as jnp
from jax import lax
from jax.sharding import PartitionSpec as P

HIGH = lax.Precision.HIGHEST


def extended(block, sides, width):
    for axis, dim in sides:
        count = lax.axis_size(axis)
        forward = [(i, i + 1) for i in range(count - 1)]
        forward.append((count - 1, 0))
        backward = [(target, source) for source, target in forward]
        low = lax.ppermute(
            lax.slice_in_dim(block, block.shape[dim] - width, None, axis=dim), axis, forward
        )
        high = lax.ppermute(lax.slice_in_dim(block, 0, width, axis=dim), axis, backward)
        block = jnp.concatenate([low, block, high], axis=dim)
    return block


def interp_table(coarse):
    fine_len = 2 * coarse
    fine_pos = jnp.arange(fine_len, dtype=jnp.float32)[:, None]
    coarse_pos = jnp.arange(coarse, dtype=jnp.float32)[None, :]
    frequency = jnp.arange(1, coarse // 2, dtype=jnp.float32)[:, None, None]
    phases = 2.0 * jnp.pi * frequency * (fine_pos / fine_len - coarse_pos / coarse)
    summed = (
        1.0
        + 2.0 * jnp.sum(jnp.cos(phases), axis=0)
        + jnp.cos(jnp.pi * coarse_pos) * jnp.cos(jnp.pi * fine_pos * coarse / fine_len)
    )
    return (summed / coarse).astype(jnp.bfloat16)


def half_targets(domains, size_x, size_y, size_z):
    index_x = domains // (size_y * size_z)
    index_y = domains // size_z % size_y
    index_z = domains % size_z
    shift_x = jnp.array([0, 1], dtype=jnp.int32)
    return (
        (index_x[:, None] + shift_x[None, :]) % size_x * size_y + index_y[:, None]
    ) * size_z + index_z[:, None]


def interpolate(planes, table_full):
    box_count, fun_count, cells = planes.shape
    coarse = table_full.shape[1]
    shaped = planes.reshape(box_count, fun_count, coarse, coarse)
    stretched = jnp.einsum(
        "bfxy,Xx->bfyX", shaped, table_full, preferred_element_type=jnp.float32
    ).astype(jnp.bfloat16)
    return jnp.einsum(
        "bfyX,Yy->bfXY", stretched, table_full, preferred_element_type=jnp.float32
    ).astype(jnp.bfloat16)


def block_density(func_blk, resp_blk, pidx_blk, weight_blk, table_full):
    fun_count = func_blk.shape[1]
    coarse = table_full.shape[1]
    fine_f = interpolate(func_blk, table_full)
    fine_r = interpolate(resp_blk, table_full)
    levels = jnp.arange(fun_count, dtype=jnp.int32)
    first_hot = (pidx_blk[0][..., None] == levels).astype(jnp.float32)
    second_hot = (pidx_blk[1][..., None] == levels).astype(jnp.float32)
    kernel_pairs = jnp.einsum(
        "bp,bpf,bpg->bfg", weight_blk, first_hot, second_hot, precision=HIGH
    ).astype(jnp.bfloat16)
    mixed_resp = jnp.einsum(
        "bfg,bgXY->bfXY", kernel_pairs, fine_r, preferred_element_type=jnp.float32
    )
    density = jnp.sum(fine_f.astype(jnp.float32) * mixed_resp, axis=1)
    halves = density.reshape(density.shape[0], 2, 2 * coarse * coarse)
    return (halves, fine_f)


def block_apply(fine_f, box_pot, table_half):
    weighted = (box_pot[:, None].astype(jnp.float32) * fine_f.astype(jnp.float32)).astype(
        jnp.bfloat16
    )
    colwise = jnp.einsum(
        "bfXY,Xx->bfYx", weighted, table_half, preferred_element_type=jnp.float32
    ).astype(jnp.bfloat16)
    result = jnp.einsum(
        "bfYx,Yy->bfxy", colwise, table_half, preferred_element_type=jnp.float32
    ).astype(jnp.bfloat16)
    return result.reshape(result.shape[0], result.shape[1], result.shape[2] * result.shape[3])


def on_device(functions, responses, box_domain, pair_index, pair_weight, kernel_xc):
    box_count, fun_count, cells = functions.shape
    coarse = math.isqrt(cells)
    fine_side = 2 * coarse
    half_cells = coarse * fine_side
    table_full = interp_table(coarse)
    table_half = table_full * 0.5
    size_x = lax.axis_size("gx")
    size_y = lax.axis_size("gy")
    size_z = lax.axis_size("gz")
    per_block = 16
    blocks = box_count // per_block
    domains = box_domain[:, 0]
    targets = half_targets(domains, size_x, size_y, size_z)

    def blocked(array):
        return array.reshape((blocks, per_block) + array.shape[1:])

    pidx_blocks = pair_index.reshape(2, blocks, per_block, pair_index.shape[2]).transpose(
        1, 0, 2, 3
    )
    first_inputs = (blocked(functions), blocked(responses), pidx_blocks, blocked(pair_weight))

    def first_keep(inputs):
        return block_density(inputs[0], inputs[1], inputs[2], inputs[3], table_full)

    halves, fine_all = lax.map(first_keep, first_inputs)
    halves = halves.reshape(box_count * 2, half_cells)
    own_y = lax.axis_index("gy")
    own_z = lax.axis_index("gz")
    target_x = targets // (size_y * size_z)
    target_y = targets // size_z % size_y
    target_z = targets % size_z
    near_y = (target_y - own_y + 1) % size_y
    near_z = (target_z - own_z + 1) % size_z
    slot_code = (target_x * 3 + near_y) * 3 + near_z
    slots = jnp.arange(9 * size_x, dtype=jnp.int32)
    one_hot = (slot_code.reshape(-1)[None, :] == slots[:, None]).astype(jnp.float32)
    beside_all = jnp.dot(one_hot, halves, precision=HIGH)
    slab = lax.psum_scatter(
        beside_all.reshape(size_x, 3, 3, half_cells).astype(jnp.bfloat16),
        "gx",
        scatter_dimension=0,
        tiled=True,
    ).astype(jnp.float32)
    padded = extended(slab[0].astype(jnp.bfloat16), (("gy", 0), ("gz", 1)), 1).astype(jnp.float32)
    density = jnp.sum(padded[0::2, 0::2].reshape(9, half_cells), axis=0)[None, :]
    potential = (kernel_xc * density).astype(jnp.bfloat16)
    neighbours = extended(potential.reshape(1, 1, half_cells), (("gy", 0), ("gz", 1)), 1)
    whole = lax.all_gather(neighbours[None], "gx", axis=0, tiled=True)
    box_rows = whole.reshape(9 * size_x, half_cells)[slot_code]
    box_pot = blocked(box_rows.reshape(box_count, fine_side, fine_side))

    def second_keep(inputs):
        return block_apply(inputs[0], inputs[1], table_half)

    applied = lax.map(second_keep, (fine_all, box_pot))
    return (applied.reshape(box_count, fun_count, cells), potential)


def solution(mesh):
    in_specs = (
        P(("gx", "gy", "gz"), None, None),
        P(("gx", "gy", "gz"), None, None),
        P(("gx", "gy", "gz"), None),
        P(None, ("gx", "gy", "gz"), None),
        P(("gx", "gy", "gz"), None),
        P(("gx", "gy", "gz"), None),
    )
    out_specs = (P(("gx", "gy", "gz"), None, None), P(("gx", "gy", "gz"), None))
    return jax.shard_map(
        on_device, mesh=mesh, in_specs=in_specs, out_specs=out_specs, check_vma=False
    )
```

profile of v0, /device:TPU:0, one launch (start us, length us, event | category | flops | bytes accessed | tf_op | source)
XLA Modules:
  0.0 341.9 jit_solution(11772122494668481576)
XLA Ops:
  10.4 3.3 cosine_reduce_fusion
  13.8 178.1 %while.22 = (s32[]{:T(128)}, f32[5,16,2,8192]{3,2,1,0:T(2,128)}, bf16[5,16,8,128,128]{4,3,2,1,0:T(8,128)(2,1)}, bf16[5,16,8,4096]{3,2,1,0:T(8,128)(2,1)}, bf16[1...) while((s32[]{:T(128)}, f32[5,16,2,8192]{3,2,1,0:T(2,128)}, ...), condition=%wide.region_3.4_spmd, body=%wide.region_1.3_spmd.sunk | while | flops 851486720 | bytes 53551720 | solution.py:119
  21.6 3.6 %copy.57 = bf16[16,8,64,128]{2,1,3,0:T(8,128)(2,1)} copy(bf16[16,8,64,128]{3,2,1,0:T(8,128)(2,1)S(1)} %convolution_convert_fusion.5) | data formatting | bytes 4194304 | tf_op jit(solution)/shard_map/while/body/eval_jaxpr/convert_element_type | solution.py:55
  25.2 7.9 %fusion.116 = f32[16,8,128,128]{3,1,2,0:T(8,128)} fusion(bf16[16,8,8,1]{2,1,3,0:T(8,128)(2,1)S(1)} %fusion.115, bf16[16,8,64,128]{2,1,3,0:T(8,128)(2,1)} %copy.57, bf16[128,64]{0,1:T(8,128)(2,1)S(1)} %get-tuple-element.270), kind=kOutput, calls=%fused_computation.4.clone.1 | convolution fusion | flops 304087040 | bytes 10504192 | tf_op jit(solution)/shard_map/while/body/eval_jaxpr/bfg,bgXY->bfXY/dot_general | solution.py:72
  35.3 7.9 %fusion.117 = (f32[16,128,128]{2,1,0:T(8,128)S(1)}, bf16[16,8,128,128]{3,2,1,0:T(8,128)(2,1)}) fusion(f32[16,8,128,128]{3,1,2,0:T(8,128)} %fusion.116, bf16[128,64]{0,1:T(8,128)(2,1)S(1)} %get-tuple-element.270, bf16[16,8,64,64]{3,2,1,0:T(8,128)(2,1)S(1)} %reshape.655), kind=kOutput, calls=%fused_computation.2.clone.1 | convolution fusion | flops 411828224 | bytes 14696448 | tf_op jit(solution)/shard_map/while/body/eval_jaxpr/bfyX,Yy->bfXY/dot_general | solution.py:56
  43.3 4.7 %bitcast_dynamic-update-slice_fusion.2 = bf16[5,16,8,128,128]{4,3,2,1,0:T(8,128)(2,1)} fusion(bf16[5,16,8,128,128]{4,3,2,1,0:T(8,128)(2,1)} %get-tuple-element.259, s32[]{:T(128)} %get-tuple-element.257, bf16[16,8,128,128]{3,2,1,0:T(8,128)(2,1)} %get-tuple-element.242), kind=kLoop, calls=%fused_computation.3.clone.1 | loop fusion | bytes 8389120 | tf_op jit(solution)/shard_map/while/body/jit(dynamic_update_index_in_dim)/dynamic_update_slice | solution.py:119
  57.2 3.6 %copy.57 = bf16[16,8,64,128]{2,1,3,0:T(8,128)(2,1)} copy(bf16[16,8,64,128]{3,2,1,0:T(8,128)(2,1)S(1)} %convolution_convert_fusion.5) | data formatting | bytes 4194304 | tf_op jit(solution)/shard_map/while/body/eval_jaxpr/convert_element_type | solution.py:55
  60.8 7.9 %fusion.116 = f32[16,8,128,128]{3,1,2,0:T(8,128)} fusion(bf16[16,8,8,1]{2,1,3,0:T(8,128)(2,1)S(1)} %fusion.115, bf16[16,8,64,128]{2,1,3,0:T(8,128)(2,1)} %copy.57, bf16[128,64]{0,1:T(8,128)(2,1)S(1)} %get-tuple-element.270), kind=kOutput, calls=%fused_computation.4.clone.1 | convolution fusion | flops 304087040 | bytes 10504192 | tf_op jit(solution)/shard_map/while/body/eval_jaxpr/bfg,bgXY->bfXY/dot_general | solution.py:72
  70.9 7.9 %fusion.117 = (f32[16,128,128]{2,1,0:T(8,128)S(1)}, bf16[16,8,128,128]{3,2,1,0:T(8,128)(2,1)}) fusion(f32[16,8,128,128]{3,1,2,0:T(8,128)} %fusion.116, bf16[128,64]{0,1:T(8,128)(2,1)S(1)} %get-tuple-element.270, bf16[16,8,64,64]{3,2,1,0:T(8,128)(2,1)S(1)} %reshape.655), kind=kOutput, calls=%fused_computation.2.clone.1 | convolution fusion | flops 411828224 | bytes 14696448 | tf_op jit(solution)/shard_map/while/body/eval_jaxpr/bfyX,Yy->bfXY/dot_general | solution.py:56
  78.8 4.7 %bitcast_dynamic-update-slice_fusion.2 = bf16[5,16,8,128,128]{4,3,2,1,0:T(8,128)(2,1)} fusion(bf16[5,16,8,128,128]{4,3,2,1,0:T(8,128)(2,1)} %get-tuple-element.259, s32[]{:T(128)} %get-tuple-element.257, bf16[16,8,128,128]{3,2,1,0:T(8,128)(2,1)} %get-tuple-element.242), kind=kLoop, calls=%fused_computation.3.clone.1 | loop fusion | bytes 8389120 | tf_op jit(solution)/shard_map/while/body/jit(dynamic_update_index_in_dim)/dynamic_update_slice | solution.py:119
  92.7 3.6 %copy.57 = bf16[16,8,64,128]{2,1,3,0:T(8,128)(2,1)} copy(bf16[16,8,64,128]{3,2,1,0:T(8,128)(2,1)S(1)} %convolution_convert_fusion.5) | data formatting | bytes 4194304 | tf_op jit(solution)/shard_map/while/body/eval_jaxpr/convert_element_type | solution.py:55
  96.3 7.9 %fusion.116 = f32[16,8,128,128]{3,1,2,0:T(8,128)} fusion(bf16[16,8,8,1]{2,1,3,0:T(8,128)(2,1)S(1)} %fusion.115, bf16[16,8,64,128]{2,1,3,0:T(8,128)(2,1)} %copy.57, bf16[128,64]{0,1:T(8,128)(2,1)S(1)} %get-tuple-element.270), kind=kOutput, calls=%fused_computation.4.clone.1 | convolution fusion | flops 304087040 | bytes 10504192 | tf_op jit(solution)/shard_map/while/body/eval_jaxpr/bfg,bgXY->bfXY/dot_general | solution.py:72
  106.5 7.9 %fusion.117 = (f32[16,128,128]{2,1,0:T(8,128)S(1)}, bf16[16,8,128,128]{3,2,1,0:T(8,128)(2,1)}) fusion(f32[16,8,128,128]{3,1,2,0:T(8,128)} %fusion.116, bf16[128,64]{0,1:T(8,128)(2,1)S(1)} %get-tuple-element.270, bf16[16,8,64,64]{3,2,1,0:T(8,128)(2,1)S(1)} %reshape.655), kind=kOutput, calls=%fused_computation.2.clone.1 | convolution fusion | flops 411828224 | bytes 14696448 | tf_op jit(solution)/shard_map/while/body/eval_jaxpr/bfyX,Yy->bfXY/dot_general | solution.py:56
  114.4 4.7 %bitcast_dynamic-update-slice_fusion.2 = bf16[5,16,8,128,128]{4,3,2,1,0:T(8,128)(2,1)} fusion(bf16[5,16,8,128,128]{4,3,2,1,0:T(8,128)(2,1)} %get-tuple-element.259, s32[]{:T(128)} %get-tuple-element.257, bf16[16,8,128,128]{3,2,1,0:T(8,128)(2,1)} %get-tuple-element.242), kind=kLoop, calls=%fused_computation.3.clone.1 | loop fusion | bytes 8389120 | tf_op jit(solution)/shard_map/while/body/jit(dynamic_update_index_in_dim)/dynamic_update_slice | solution.py:119
  128.3 3.6 %copy.57 = bf16[16,8,64,128]{2,1,3,0:T(8,128)(2,1)} copy(bf16[16,8,64,128]{3,2,1,0:T(8,128)(2,1)S(1)} %convolution_convert_fusion.5) | data formatting | bytes 4194304 | tf_op jit(solution)/shard_map/while/body/eval_jaxpr/convert_element_type | solution.py:55
  131.9 7.9 %fusion.116 = f32[16,8,128,128]{3,1,2,0:T(8,128)} fusion(bf16[16,8,8,1]{2,1,3,0:T(8,128)(2,1)S(1)} %fusion.115, bf16[16,8,64,128]{2,1,3,0:T(8,128)(2,1)} %copy.57, bf16[128,64]{0,1:T(8,128)(2,1)S(1)} %get-tuple-element.270), kind=kOutput, calls=%fused_computation.4.clone.1 | convolution fusion | flops 304087040 | bytes 10504192 | tf_op jit(solution)/shard_map/while/body/eval_jaxpr/bfg,bgXY->bfXY/dot_general | solution.py:72
  142.1 7.9 %fusion.117 = (f32[16,128,128]{2,1,0:T(8,128)S(1)}, bf16[16,8,128,128]{3,2,1,0:T(8,128)(2,1)}) fusion(f32[16,8,128,128]{3,1,2,0:T(8,128)} %fusion.116, bf16[128,64]{0,1:T(8,128)(2,1)S(1)} %get-tuple-element.270, bf16[16,8,64,64]{3,2,1,0:T(8,128)(2,1)S(1)} %reshape.655), kind=kOutput, calls=%fused_computation.2.clone.1 | convolution fusion | flops 411828224 | bytes 14696448 | tf_op jit(solution)/shard_map/while/body/eval_jaxpr/bfyX,Yy->bfXY/dot_general | solution.py:56
  150.0 4.7 %bitcast_dynamic-update-slice_fusion.2 = bf16[5,16,8,128,128]{4,3,2,1,0:T(8,128)(2,1)} fusion(bf16[5,16,8,128,128]{4,3,2,1,0:T(8,128)(2,1)} %get-tuple-element.259, s32[]{:T(128)} %get-tuple-element.257, bf16[16,8,128,128]{3,2,1,0:T(8,128)(2,1)} %get-tuple-element.242), kind=kLoop, calls=%fused_computation.3.clone.1 | loop fusion | bytes 8389120 | tf_op jit(solution)/shard_map/while/body/jit(dynamic_update_index_in_dim)/dynamic_update_slice | solution.py:119
  163.9 3.6 %copy.57 = bf16[16,8,64,128]{2,1,3,0:T(8,128)(2,1)} copy(bf16[16,8,64,128]{3,2,1,0:T(8,128)(2,1)S(1)} %convolution_convert_fusion.5) | data formatting | bytes 4194304 | tf_op jit(solution)/shard_map/while/body/eval_jaxpr/convert_element_type | solution.py:55
  167.5 7.9 %fusion.116 = f32[16,8,128,128]{3,1,2,0:T(8,128)} fusion(bf16[16,8,8,1]{2,1,3,0:T(8,128)(2,1)S(1)} %fusion.115, bf16[16,8,64,128]{2,1,3,0:T(8,128)(2,1)} %copy.57, bf16[128,64]{0,1:T(8,128)(2,1)S(1)} %get-tuple-element.270), kind=kOutput, calls=%fused_computation.4.clone.1 | convolution fusion | flops 304087040 | bytes 10504192 | tf_op jit(solution)/shard_map/while/body/eval_jaxpr/bfg,bgXY->bfXY/dot_general | solution.py:72
  177.6 7.9 %fusion.117 = (f32[16,128,128]{2,1,0:T(8,128)S(1)}, bf16[16,8,128,128]{3,2,1,0:T(8,128)(2,1)}) fusion(f32[16,8,128,128]{3,1,2,0:T(8,128)} %fusion.116, bf16[128,64]{0,1:T(8,128)(2,1)S(1)} %get-tuple-element.270, bf16[16,8,64,64]{3,2,1,0:T(8,128)(2,1)S(1)} %reshape.655), kind=kOutput, calls=%fused_computation.2.clone.1 | convolution fusion | flops 411828224 | bytes 14696448 | tf_op jit(solution)/shard_map/while/body/eval_jaxpr/bfyX,Yy->bfXY/dot_general | solution.py:56
  185.5 4.7 %bitcast_dynamic-update-slice_fusion.2 = bf16[5,16,8,128,128]{4,3,2,1,0:T(8,128)(2,1)} fusion(bf16[5,16,8,128,128]{4,3,2,1,0:T(8,128)(2,1)} %get-tuple-element.259, s32[]{:T(128)} %get-tuple-element.257, bf16[16,8,128,128]{3,2,1,0:T(8,128)(2,1)} %get-tuple-element.242), kind=kLoop, calls=%fused_computation.3.clone.1 | loop fusion | bytes 8389120 | tf_op jit(solution)/shard_map/while/body/jit(dynamic_update_index_in_dim)/dynamic_update_slice | solution.py:119
  191.9 7.7 %reshape.649 = f32[160,8192,1,1]{1,0,2,3:T(8,128)} reshape(f32[5,16,2,8192]{3,2,1,0:T(2,128)} %get-tuple-element.72) | data formatting | bytes 10485760 | tf_op jit(solution)/shard_map/reshape | solution.py:120
  199.6 4.9 %convolution_convert_fusion.3 = bf16[4,3,3,8192]{3,0,2,1:T(4,128)(2,1)S(1)} fusion(f32[160,8192,1,1]{1,0,2,3:T(8,128)} %reshape.649, s32[4,3,3]{0,2,1:T(4,128)S(1)} %multiply_add_fusion, s32[160]{0:T(256)S(1)} %fusion.68), kind=kOutput, calls=%fused_computation.44 | convolution fusion | flops 566531712 | bytes 5833488 | tf_op jit(solution)/shard_map/dot_general | solution.py:131
  206.5 50.9 %all-reduce.3.cloned.1.call-done = bf16[4,3,3,8192]{3,2,1,0:T(4,128)(2,1)} async-done(((bf16[4,3,3,8192]{3,2,1,0:T(4,128)(2,1)}), bf16[4,3,3,8192]{3,2,1,0:T(4,128)(2,1)}) %all-reduce.3.cloned.1.call-update) | async-done | bytes 589840
  278.8 12.5 %all-gather = bf16[12,3,8192]{2,1,0:T(4,128)(2,1)S(1)} all-gather(bf16[3,3,8192]{2,1,0:T(4,128)(2,1)S(1)} %pad_maximum_fusion.2), channel_id=2, replica_groups=mesh['gx'=4,'gy'=4,'gz'=2] {'gx'}, dimensions={0}, use_global_device_ids=true | all-gather | bytes 737280 | tf_op jit(solution)/shard_map/all_gather | solution.py:142
  297.2 37.8 %while.23 = (s32[]{:T(128)}, bf16[5,16,8,4096]{3,2,1,0:T(8,128)(2,1)}, bf16[5,16,128,128]{3,2,1,0:T(8,128)(2,1)}, bf16[5,16,8,128,128]{4,3,2,1,0:T(8,128)(2,1)}, bf16[128,64]{0,1:T(8,128)(2,1)S(1)}, /*index=5*/s32[]{:T(128)}) while((s32[]{:T(128)}, bf16[5,16,8,4096]{3,2,1,0:T(8,128)(2,1)}, bf16[5,16,128,128]{3,2,1,0:T(8,128)(2,1)}, ...), condition=%wide.region_7.8_spmd, body=%wide.region_6.7_spmd.sunk | while | flops 410779648 | bytes 12092489 | solution.py:149
  298.3 3.7 %fusion.122 = bf16[16,8,64,64]{3,2,1,0:T(8,128)(2,1)S(1)} fusion(bf16[5,16,8,128,128]{4,3,2,1,0:T(8,128)(2,1)} %get-tuple-element.290, s32[]{:T(128)} %get-tuple-element.281, f32[16,128,128]{2,1,0:T(8,128)S(1)} %bitcast_convert_fusion.2, bf16[128,64]{0,1:T(8,128)(2,1)S(1)} %get-tuple-element.291), kind=kOutput, calls=%fused_computation.39.clone.1 | convolution fusion | flops 410517504 | bytes 6324736 | tf_op jit(solution)/shard_map/while/body/eval_jaxpr/bfYx,Yy->bfxy/dot_general | solution.py:87
  305.9 3.7 %fusion.122 = bf16[16,8,64,64]{3,2,1,0:T(8,128)(2,1)S(1)} fusion(bf16[5,16,8,128,128]{4,3,2,1,0:T(8,128)(2,1)} %get-tuple-element.290, s32[]{:T(128)} %get-tuple-element.281, f32[16,128,128]{2,1,0:T(8,128)S(1)} %bitcast_convert_fusion.2, bf16[128,64]{0,1:T(8,128)(2,1)S(1)} %get-tuple-element.291), kind=kOutput, calls=%fused_computation.39.clone.1 | convolution fusion | flops 410517504 | bytes 6324736 | tf_op jit(solution)/shard_map/while/body/eval_jaxpr/bfYx,Yy->bfxy/dot_general | solution.py:87
  313.5 3.7 %fusion.122 = bf16[16,8,64,64]{3,2,1,0:T(8,128)(2,1)S(1)} fusion(bf16[5,16,8,128,128]{4,3,2,1,0:T(8,128)(2,1)} %get-tuple-element.290, s32[]{:T(128)} %get-tuple-element.281, f32[16,128,128]{2,1,0:T(8,128)S(1)} %bitcast_convert_fusion.2, bf16[128,64]{0,1:T(8,128)(2,1)S(1)} %get-tuple-element.291), kind=kOutput, calls=%fused_computation.39.clone.1 | convolution fusion | flops 410517504 | bytes 6324736 | tf_op jit(solution)/shard_map/while/body/eval_jaxpr/bfYx,Yy->bfxy/dot_general | solution.py:87
  321.0 3.7 %fusion.122 = bf16[16,8,64,64]{3,2,1,0:T(8,128)(2,1)S(1)} fusion(bf16[5,16,8,128,128]{4,3,2,1,0:T(8,128)(2,1)} %get-tuple-element.290, s32[]{:T(128)} %get-tuple-element.281, f32[16,128,128]{2,1,0:T(8,128)S(1)} %bitcast_convert_fusion.2, bf16[128,64]{0,1:T(8,128)(2,1)S(1)} %get-tuple-element.291), kind=kOutput, calls=%fused_computation.39.clone.1 | convolution fusion | flops 410517504 | bytes 6324736 | tf_op jit(solution)/shard_map/while/body/eval_jaxpr/bfYx,Yy->bfxy/dot_general | solution.py:87
  328.6 3.7 %fusion.122 = bf16[16,8,64,64]{3,2,1,0:T(8,128)(2,1)S(1)} fusion(bf16[5,16,8,128,128]{4,3,2,1,0:T(8,128)(2,1)} %get-tuple-element.290, s32[]{:T(128)} %get-tuple-element.281, f32[16,128,128]{2,1,0:T(8,128)S(1)} %bitcast_convert_fusion.2, bf16[128,64]{0,1:T(8,128)(2,1)S(1)} %get-tuple-element.291), kind=kOutput, calls=%fused_computation.39.clone.1 | convolution fusion | flops 410517504 | bytes 6324736 | tf_op jit(solution)/shard_map/while/body/eval_jaxpr/bfYx,Yy->bfxy/dot_general | solution.py:87
  (128 shorter events, 108.7 us)
Async XLA Ops:
  7.2 250.2 %all-reduce.3.cloned.1.call-start = ((), (), s32[]{:S(2)}) async-start(), calls=%async_computation | async-start | bytes 1572864
  199.6 6.3 %copy-start.2 = (u32[32]{0:T(128)S(1)}, u32[32]{0:T(128)}, u32[]{:S(2)}) copy-start(u32[32]{0:T(128)} %constant.191) | copy-start | bytes 388
  204.5 66.4 %copy-start.1 = (f32[1,8192]{1,0:T(1,128)S(1)}, f32[1,8192]{1,0:T(1,128)}, u32[]{:S(2)}) copy-start(f32[1,8192]{1,0:T(1,128)} %param.16) | copy-start | bytes 98308
  259.0 6.8 %collective-permute-start = (bf16[1,3,8192]{2,1,0:T(4,128)(2,1)S(1)}, bf16[1,3,8192]{2,1,0:T(4,128)(2,1)S(1)}, u32[]{:S(2)}, u32[]{:S(2)}) collective-permute-start(bf16[1,3,8192]{2,1,0:T(4,128)(2,1)S(1)} %get-tuple-element.149), channel_id=1, source_target_pairs={{0,2},{2,4},{4,6},{6,0},{1,3},{3,5},{5,7},{7,1},{8,10},{10,12},{12... | collective-permute-start | bytes 147464 | tf_op jit(solution)/shard_map/ppermute | solution.py:17
  260.5 5.3 %collective-permute-start.1 = (bf16[1,3,8192]{2,1,0:T(4,128)(2,1)S(1)}, bf16[1,3,8192]{2,1,0:T(4,128)(2,1)S(1)}, u32[]{:S(2)}, u32[]{:S(2)}) collective-permute-start(bf16[1,3,8192]{2,1,0:T(4,128)(2,1)S(1)} %get-tuple-element.150), channel_id=1, source_target_pairs={{2,0},{4,2},{6,4},{0,6},{3,1},{5,3},{7,5},{1,7},{10,8},{12,10},{14... | collective-permute-start | bytes 147464 | tf_op jit(solution)/shard_map/ppermute | solution.py:20
  266.3 1.5 collective-permute-start.2
  266.4 1.6 collective-permute-start.3
  270.9 23.1 %copy-start = (bf16[1,8192]{1,0:T(2,128)(2,1)}, bf16[1,8192]{1,0:T(2,128)(2,1)S(1)}, u32[]{:S(2)}) copy-start(bf16[1,8192]{1,0:T(2,128)(2,1)S(1)} %multiply_convert_fusion) | copy-start | bytes 49156
  271.0 5.8 %collective-permute-start.4 = (bf16[1,1,8192]{2,1,0:T(2,128)(2,1)S(1)}, bf16[1,1,8192]{2,1,0:T(2,128)(2,1)S(1)}, u32[]{:S(2)}, u32[]{:S(2)}) collective-permute-start(bf16[1,1,8192]{2,1,0:T(2,128)(2,1)S(1)} %bitcast.124), channel_id=1, source_target_pairs={{0,2},{2,4},{4,6},{6,0},{1,3},{3,5},{5,7},{7,1},{8,10},{10,12},{12... | collective-permute-start | bytes 49160 | tf_op jit(solution)/shard_map/ppermute | solution.py:17
  271.9 4.8 %collective-permute-start.5 = (bf16[1,1,8192]{2,1,0:T(2,128)(2,1)S(1)}, bf16[1,1,8192]{2,1,0:T(2,128)(2,1)S(1)}, u32[]{:S(2)}, u32[]{:S(2)}) collective-permute-start(bf16[1,1,8192]{2,1,0:T(2,128)(2,1)S(1)} %bitcast.125), channel_id=1, source_target_pairs={{2,0},{4,2},{6,4},{0,6},{3,1},{5,3},{7,5},{1,7},{10,8},{12,10},{14... | collective-permute-start | bytes 49160 | tf_op jit(solution)/shard_map/ppermute | solution.py:20
  276.9 1.4 collective-permute-start.6
  277.0 1.4 collective-permute-start.7
Sparse Core Ops, SparseCore 0:
  206.0 51.3 all-reduce.2
where the time goes:
time: 343 us; the launch traced here: 342 us
  local copies, waits for them, and re-layouts  123 us (36%)
  matrix products  115 us (34%)
  waiting for transfers between devices  55.8 us (16%)
  between operations  14.2 us (4%)
  blocking collectives  12.5 us (4%)
  other arithmetic  11.7 us (3%)
  starting transfers between devices  8.93 us (3%)
    unnamed x2, waiting for transfers between devices  50.9 us
    dot_general x5, matrix products, interpolate(): jnp.einsum('bfyX,Yy->bfXY', stretched, table_full, preferred_element_type...  39.7 us
    dot_general x5, matrix products, block_density(): jnp.einsum('bfg,bgXY->bfXY', kernel_pairs, fine_r, preferred_element_type...  39.3 us
    dynamic_update_slice x10, local copies, waits for them, and re-layouts, on_device(): halves, fine_all = lax.map(first_keep, first_inputs)  28.9 us
    reshape x10, local copies, waits for them, and re-layouts, interpolate(): shaped = planes.reshape(box_count, fun_count, coarse, coarse)  27.8 us
    dot_general x5, matrix products, block_apply(): jnp.einsum('bfYx,Yy->bfxy', colwise, table_half, preferred_element_type=j...  18.4 us
    convert_element_type x5, local copies, waits for them, and re-layouts, interpolate(): stretched = jnp.einsum('bfxy,Xx->bfyX', shaped, table_full, preferred_ele...  18 us
    all_gather x1, blocking collectives, on_device(): whole = lax.all_gather(neighbours[None], 'gx', axis=0, tiled=True)  12.5 us
  transfers between devices with their start and end apart: 9, of which 7 were waited for; matrix products, arithmetic and copies ran while one was open for 1% of the time, Pallas kernels for 0%

commit v1 on v0

v1 whole, which is shorter than its diff:
```python
import functools
import math

import jax
import jax.numpy as jnp
import numpy as np
from jax import lax
from jax.experimental import pallas as pl
from jax.experimental.pallas import tpu as pltpu
from jax.sharding import PartitionSpec as P

MESH = pl.DeviceIdType.MESH
F32 = jnp.float32
BF16 = jnp.bfloat16
STEP_BOXES = 16


def interp_table(coarse):
    fine = 2 * coarse
    m = np.arange(fine, dtype=np.float64)[:, None]
    n = np.arange(coarse, dtype=np.float64)[None, :]
    k = np.arange(1, coarse // 2, dtype=np.float64)[:, None, None]
    total = 1.0 + 2.0 * np.sum(np.cos(2.0 * np.pi * k * (m / fine - n / coarse)), axis=0)
    total = total + np.cos(np.pi * n) * np.cos(np.pi * m * coarse / fine)
    return total / coarse


def tables(coarse):
    odd = interp_table(coarse)[1::2]
    order = np.concatenate([np.arange(0, coarse, 2), np.arange(1, coarse, 2)])
    along_x = odd[order][:, order]
    quad = np.eye(4)
    rows = np.array(
        [4 * jj + 2 * p + xp for xp in range(2) for p in range(2) for jj in range(coarse // 4)]
    )
    cols = np.array([2 * y + yp for yp in range(2) for y in range(coarse)])
    row_pick = np.zeros((coarse, coarse))
    row_pick[np.arange(coarse), rows] = 1.0
    col_pick = np.zeros((2 * coarse, 2 * coarse))
    col_pick[cols, np.arange(2 * coarse)] = 1.0

    def low(array):
        return jnp.asarray(np.ascontiguousarray(array), F32).astype(BF16)

    return {
        "ax": low(along_x),
        "axt": low(along_x.T),
        "yup": low(np.kron(quad, odd.T)),
        "ydown": low(np.kron(quad, odd)),
        "row": low(row_pick),
        "rowt": low(row_pick.T),
        "col": low(col_pick),
        "colt": low(col_pick.T),
    }


def dot(a, b):
    return jnp.dot(a, b, preferred_element_type=F32)


def density_kernel(
    coarse, steps, slots, bd, func, resp, ax, yup, fe, fo, part, rm, sf, sr, me, mo, acc
):
    step = pl.program_id(0)
    half = coarse // 2
    quarter = coarse // 4
    lanes = 2 * coarse
    left = lax.broadcasted_iota(jnp.int32, (half, lanes), 1) < coarse
    left_all = lax.broadcasted_iota(jnp.int32, (lanes, lanes), 1) < coarse

    @pl.when(step == 0)
    def _():
        acc[...] = jnp.zeros_like(acc)

    width = 512
    for c in range(0, coarse * coarse, width):
        rm[:, c : c + width] = dot(bd[...], resp[:, c : c + width])

    def pair(i, carry):
        r0 = pl.multiple_of(i * 16, 16)
        g0 = i * 4
        for src, s, even, odd, at in ((func, sf, fe, fo, g0), (rm, sr, me, mo, 0)):
            for j in range(half):
                s[pl.ds(j, 16, stride=half), :] = src[
                    pl.ds(r0, 16), j * lanes : (j + 1) * lanes
                ].astype(F32)
            for g in range(4):
                t = [s[(4 * g + k) * half : (4 * g + k + 1) * half, :] for k in range(4)]
                evens, odds = [], []
                for k in (0, 2):
                    evens.append(jnp.where(left, t[k], pltpu.roll(t[k + 1], coarse, 1)))
                    odds.append(jnp.where(left, pltpu.roll(t[k], coarse, 1), t[k + 1]))
                x = jnp.concatenate(
                    [jnp.concatenate(evens, axis=1), jnp.concatenate(odds, axis=1)], axis=0
                ).astype(BF16)
                up = dot(ax[...], x).astype(BF16)
                even[at + g, 0:coarse, :] = x
                even[at + g, coarse:lanes, :] = up
                both = jnp.concatenate([x, up], axis=0)
                odd[at + g, :, :] = dot(both, yup[...]).astype(BF16)
        for b in range(2):
            sums = []
            for left_src, right_src in ((fe, me), (fo, mo)):
                total = None
                for g in (2 * b, 2 * b + 1):
                    prod = left_src[g0 + g].astype(F32) * right_src[g].astype(F32)
                    prod = prod[:, :lanes] + prod[:, lanes:]
                    total = prod if total is None else total + prod
                sums.append(total + pltpu.roll(total, coarse, 1))
            d = jnp.where(left_all, sums[0], sums[1])
            at = (step * STEP_BOXES + 2 * i + b) * 2
            for q in range(2):
                slot = slots[at + q]
                for c in range(4):
                    acc[slot, c * quarter : (c + 1) * quarter, :] += d[
                        c * half + q * quarter : c * half + (q + 1) * quarter, :
                    ]
        return carry

    lax.fori_loop(0, STEP_BOXES // 2, pair, 0)

    @pl.when(step == steps - 1)
    def _():
        part[...] = acc[...].astype(BF16)


def exchange_kernel(
    sizes, shifts, own, part, kxc, row, rowt, col, colt, ve, vo, out, got, pot, back, s1, r1, s2, r2
):
    coarse = kxc.shape[0]
    me = [lax.axis_index(name) for name in ("gx", "gy", "gz")]

    def device(shift, sign):
        return tuple(
            lax.rem(me[a] + (sign * shift[a]) % sizes[a], sizes[a]) for a in range(3)
        )

    others = [k for k in range(len(shifts)) if k != own]
    barrier = pltpu.get_barrier_semaphore()
    for k in others:
        pl.semaphore_signal(
            barrier, inc=1, device_id=device(shifts[k], -1), device_id_type=MESH
        )
    pl.semaphore_wait(barrier, len(others))
    first, second = {}, {}
    for k in others:
        first[k] = pltpu.make_async_remote_copy(
            src_ref=part.at[k],
            dst_ref=got.at[k],
            send_sem=s1.at[k],
            recv_sem=r1.at[k],
            device_id=device(shifts[k], 1),
            device_id_type=MESH,
        )
        first[k].start()
    high = lax.Precision.HIGHEST
    by_col = jnp.dot(kxc[...], col[...].astype(F32), precision=high)
    scale = jnp.dot(row[...].astype(F32), by_col, precision=high)
    total = part[own].astype(F32)
    for k in others:
        first[k].wait_recv()
        total = total + got[k].astype(F32)
    value = (scale * total).astype(BF16)
    pot[...] = value
    for k in others:
        second[k] = pltpu.make_async_remote_copy(
            src_ref=pot,
            dst_ref=back.at[k],
            send_sem=s2.at[k],
            recv_sem=r2.at[k],
            device_id=device(shifts[k], -1),
            device_id_type=MESH,
        )
        second[k].start()
    by_col = dot(value, colt[...]).astype(BF16)
    out[...] = dot(rowt[...], by_col).astype(BF16)
    left = lax.broadcasted_iota(jnp.int32, value.shape, 1) < coarse

    def spread(k, block):
        block = block.astype(F32)
        turned = pltpu.roll(block, coarse, 1)
        ve[k] = jnp.where(left, block, turned).astype(BF16)
        vo[k] = jnp.where(left, turned, block).astype(BF16)

    spread(own, value)
    for k in others:
        second[k].wait_recv()
        spread(k, back[k])
    for k in others:
        first[k].wait_send()
        second[k].wait_send()


def apply_kernel(coarse, slots, fe, fo, ve, vo, axt, ydown, out, s):
    step = pl.program_id(0)
    half = coarse // 2
    quarter = coarse // 4
    lanes = 2 * coarse
    left = lax.broadcasted_iota(jnp.int32, (half, lanes), 1) < coarse

    def pair(i, carry):
        r0 = pl.multiple_of(i * 16, 16)
        g0 = i * 4
        for b in range(2):
            at = (step * STEP_BOXES + 2 * i + b) * 2
            pieces = []
            for v in (ve, vo):
                rows = []
                for c in range(4):
                    for q in range(2):
                        rows.append(v[slots[at + q], c * quarter : (c + 1) * quarter, :])
                plane = jnp.concatenate(rows, axis=0)
                pieces.append(jnp.concatenate([plane, plane], axis=1))
            for g in (2 * b, 2 * b + 1):
                we = fe[g0 + g] * pieces[0]
                wo = fo[g0 + g] * pieces[1]
                z = we.astype(F32) + dot(wo, ydown[...])
                down = dot(axt[...], z[coarse:].astype(BF16))
                res = (z[:coarse] + down) * 0.25
                for k in (0, 2):
                    e = res[:half, k * coarse : (k + 2) * coarse]
                    o = res[half:, k * coarse : (k + 2) * coarse]
                    base = (4 * g + k) * half
                    s[base : base + half, :] = jnp.where(left, e, pltpu.roll(o, coarse, 1))
                    s[base + half : base + 2 * half, :] = jnp.where(
                        left, pltpu.roll(e, coarse, 1), o
                    )
        for j in range(half):
            out[pl.ds(r0, 16), j * lanes : (j + 1) * lanes] = s[
                pl.ds(j, 16, stride=half), :
            ].astype(BF16)
        return carry

    lax.fori_loop(0, STEP_BOXES // 2, pair, 0)


def on_device(sizes, functions, responses, box_domain, pair_index, pair_weight, kernel_xc):
    boxes, funs, cells = functions.shape
    coarse = math.isqrt(cells)
    lanes = 2 * coarse
    size_x, size_y, size_z = sizes
    near = (min(4, size_x), min(2, size_y), min(3, size_z))
    shifts = [
        (kx - 2, ky - 1, kz - 1)
        for kx in range(near[0])
        for ky in range(near[1])
        for kz in range(near[2])
    ]
    own = [k for k, sh in enumerate(shifts) if all(d % n == 0 for d, n in zip(sh, sizes))][0]
    count = len(shifts)
    t = tables(coarse)

    domain = box_domain[:, 0]
    tx = domain // (size_y * size_z)
    ty = domain // size_z % size_y
    tz = domain % size_z
    kx = (tx[:, None] + jnp.arange(2, dtype=jnp.int32) - lax.axis_index("gx") + 2) % size_x
    ky = (ty - lax.axis_index("gy") + 1) % size_y
    kz = (tz - lax.axis_index("gz") + 1) % size_z
    slots = (kx * near[1] + ky[:, None]) * near[2] + kz[:, None]
    slots = jnp.clip(slots, 0, count - 1).astype(jnp.int32).reshape(-1)

    rows = STEP_BOXES * funs
    first, second = pair_index[0], pair_index[1]
    f_of = jnp.arange(funs, dtype=jnp.int32)
    lane = jnp.arange(rows, dtype=jnp.int32)
    weight_f = jnp.where(first[:, None, :] == f_of[None, :, None], pair_weight[:, None, :], 0.0)
    same = second[:, None, :, None] == (lane % funs)[None, None, None, :]
    mixed = jnp.sum(jnp.where(same, weight_f[..., None], 0.0), axis=2)
    here = (jnp.arange(boxes, dtype=jnp.int32) % STEP_BOXES)[:, None] == (lane // funs)[None, :]
    bd = jnp.where(here[:, None, :], mixed, 0.0).astype(BF16).reshape(boxes * funs, rows)

    steps = boxes // STEP_BOXES
    groups = STEP_BOXES * funs // 4

    def whole(shape):
        return pl.BlockSpec(shape, lambda i, *_: (0,) * len(shape))

    fe, fo, part = pl.pallas_call(
        functools.partial(density_kernel, coarse, steps),
        grid_spec=pltpu.PrefetchScalarGridSpec(
            num_scalar_prefetch=1,
            grid=(steps,),
            in_specs=[
                pl.BlockSpec((rows, rows), lambda i, *_: (i, 0)),
                pl.BlockSpec((rows, cells), lambda i, *_: (i, 0)),
                pl.BlockSpec((rows, cells), lambda i, *_: (i, 0)),
                whole((coarse, coarse)),
                whole((4 * coarse, 4 * coarse)),
            ],
            out_specs=[
                pl.BlockSpec((groups, lanes, 4 * coarse), lambda i, *_: (i, 0, 0)),
                pl.BlockSpec((groups, lanes, 4 * coarse), lambda i, *_: (i, 0, 0)),
                whole((count, coarse, lanes)),
            ],
            scratch_shapes=[
                pltpu.VMEM((rows, cells), F32),
                pltpu.VMEM((16 * coarse // 2, lanes), F32),
                pltpu.VMEM((16 * coarse // 2, lanes), F32),
                pltpu.VMEM((4, lanes, 4 * coarse), BF16),
                pltpu.VMEM((4, lanes, 4 * coarse), BF16),
                pltpu.VMEM((count, coarse, lanes), F32),
            ],
        ),
        out_shape=[
            jax.ShapeDtypeStruct((steps * groups, lanes, 4 * coarse), BF16),
            jax.ShapeDtypeStruct((steps * groups, lanes, 4 * coarse), BF16),
            jax.ShapeDtypeStruct((count, coarse, lanes), BF16),
        ],
        name="density",
    )(
        slots,
        bd,
        functions.reshape(boxes * funs, cells),
        responses.reshape(boxes * funs, cells),
        t["ax"],
        t["yup"],
    )

    vm = pl.BlockSpec(memory_space=pltpu.VMEM)
    block = (count, coarse, lanes)
    ve, vo, potential = pl.pallas_call(
        functools.partial(exchange_kernel, sizes, shifts, own),
        in_specs=[vm] * 6,
        out_specs=[vm] * 3,
        out_shape=[
            jax.ShapeDtypeStruct(block, BF16),
            jax.ShapeDtypeStruct(block, BF16),
            jax.ShapeDtypeStruct((coarse, lanes), BF16),
        ],
        scratch_shapes=[
            pltpu.VMEM(block, BF16),
            pltpu.VMEM((coarse, lanes), BF16),
            pltpu.VMEM(block, BF16),
        ]
        + [pltpu.SemaphoreType.DMA((count,))] * 4,
        compiler_params=pltpu.CompilerParams(collective_id=0, has_side_effects=True),
        name="exchange",
    )(part, kernel_xc.reshape(coarse, lanes), t["row"], t["rowt"], t["col"], t["colt"])

    applied = pl.pallas_call(
        functools.partial(apply_kernel, coarse),
        grid_spec=pltpu.PrefetchScalarGridSpec(
            num_scalar_prefetch=1,
            grid=(steps,),
            in_specs=[
                pl.BlockSpec((groups, lanes, 4 * coarse), lambda i, *_: (i, 0, 0)),
                pl.BlockSpec((groups, lanes, 4 * coarse), lambda i, *_: (i, 0, 0)),
                whole(block),
                whole(block),
                whole((coarse, coarse)),
                whole((4 * coarse, 4 * coarse)),
            ],
            out_specs=pl.BlockSpec((rows, cells), lambda i, *_: (i, 0)),
            scratch_shapes=[pltpu.VMEM((16 * coarse // 2, lanes), F32)],
        ),
        out_shape=jax.ShapeDtypeStruct((boxes * funs, cells), BF16),
        name="apply",
    )(slots, fe, fo, ve, vo, t["axt"], t["ydown"])
    return applied.reshape(boxes, funs, cells), potential.reshape(1, coarse * lanes)


def solution(mesh):
    sizes = tuple(mesh.shape[name] for name in ("gx", "gy", "gz"))
    over = ("gx", "gy", "gz")
    in_specs = (
        P(over, None, None),
        P(over, None, None),
        P(over, None),
        P(None, over, None),
        P(over, None),
        P(over, None),
    )
    out_specs = (P(over, None, None), P(over, None))
    return jax.shard_map(
        functools.partial(on_device, sizes),
        mesh=mesh,
        in_specs=in_specs,
        out_specs=out_specs,
        check_vma=False,
    )
```

time: 343 us -> 116 us (0.34)
  local copies, waits for them, and re-layouts: 123 us -> 2.92 us
  matrix products: 115 us -> 0 us
  Pallas kernels: 0 us -> 107 us
  waiting for transfers between devices: 55.8 us -> 0 us
  between operations: 14.2 us -> 0.72 us
  blocking collectives: 12.5 us -> 0 us
  starting transfers between devices: 8.93 us -> 0 us
  other arithmetic: 11.7 us -> 5.28 us
    dot_general x26 -> x0, matrix products: 115 us -> none  [the longest x5 39.7 us: interpolate(): jnp.einsum('bfyX,Yy->bfXY', stretched, table_full, preferred_element_type...]
    pallas_call x0 -> x3, Pallas kernels: none -> 107 us  [the longest x1 52.2 us: on_device(): pl.pallas_call(functools.partial(density_kernel, coarse, steps), grid_spe...]
    unnamed x2 -> x0, waiting for transfers between devices: 50.9 us -> none
    reshape x12 -> x0, local copies, waits for them, and re-layouts: 35.9 us -> none  [the longest x10 27.8 us: interpolate(): shaped = planes.reshape(box_count, fun_count, coarse, coarse)]
    dynamic_update_slice x15 -> x0, local copies, waits for them, and re-layouts: 34.1 us -> none  [the longest x10 28.9 us: on_device(): halves, fine_all = lax.map(first_keep, first_inputs)]
    convert_element_type x7 -> x0, local copies, waits for them, and re-layouts: 21 us -> none  [the longest x5 18 us: interpolate(): stretched = jnp.einsum('bfxy,Xx->bfyX', shaped, table_full, preferred_ele...]
    all_gather x1 -> x0, blocking collectives: 12.5 us -> none  [on_device(): whole = lax.all_gather(neighbours[None], 'gx', axis=0, tiled=True)]
    broadcast_in_dim x10 -> x0, local copies, waits for them, and re-layouts: 11.3 us -> none  [the longest x5 8.38 us: on_device(): applied = lax.map(second_keep, (fine_all, box_pot))]
  transfers between devices with their start and end apart: 9 -> 0, of which waited for: 7 -> 0; matrix products, arithmetic and copies ran while one was open for 1% -> 0% of each run, Pallas kernels for 0% -> 0%
where the time goes in v1:
time: 116 us
  Pallas kernels  107 us (92%)
  other arithmetic  5.28 us (5%)
  local copies, waits for them, and re-layouts  2.92 us (3%)
    pallas_call x1, Pallas kernels, on_device(): pl.pallas_call(functools.partial(density_kernel, coarse, steps), grid_spe...  52.2 us
    pallas_call x1, Pallas kernels, on_device(): pl.pallas_call(functools.partial(apply_kernel, coarse), grid_spec=pltpu.P...  33.1 us
    pallas_call x1, Pallas kernels, on_device(): pl.pallas_call(functools.partial(exchange_kernel, sizes, shifts, own), in...  21.6 us
    reduce_sum x1, other arithmetic, on_device(): mixed = jnp.sum(jnp.where(same, weight_f[..., None], 0.0), axis=2)  2.76 us

profile of v1, /device:TPU:0, one launch (start us, length us, event | category | flops | bytes accessed | tf_op | source)
XLA Modules:
  0.0 115.8 jit_solution(14629294113504086112)
XLA Ops:
  0.7 0.7 fusion.14
  1.4 0.1 broadcast_compare_fusion.1
  1.4 0.7 slice_bitcast_fusion.1
  2.2 0.1 copy.22
  2.3 0.1 subtract_add_fusion
  2.3 0.1 add.119
  2.5 0.1 copy.23
  2.6 0.1 add.125
  2.6 0.1 add.126
  2.8 0.1 add.132
  2.9 0.1 add.133
  3.0 0.6 add_clamp_fusion.slots
  3.6 0.8 copy.24
  4.4 0.3 broadcast_compare_fusion
  4.8 2.8 %select_reduce_fusion = bf16[80,8,128]{2,1,0:T(8,128)(2,1)S(1)} fusion(f32[80,8,24]{2,1,0:T(8,128)S(1)} %fusion, pred[80,24,128]{2,1,0:T(8,128)(4,1)S(1)} %broadcast_compare_fusion), kind=kLoop, calls=%fused_computation | loop fusion | flops 3850240 | bytes 471040 | tf_op jit(solution)/shard_map/reduce_sum | solution.py:269
  7.5 0.7 fusion.1.bd
  8.3 52.2 %density.1 = (bf16[160,128,256]{2,1,0:T(8,128)(2,1)}, bf16[160,128,256]{2,1,0:T(8,128)(2,1)}, bf16[16,64,128]{2,1,0:T(8,128)(2,1)}) custom-call(s32[160]{0:T(256)} %add_clamp_fusion.slots, bf16[640,128]{1,0:T(8,128)(2,1)} %fusion.1.bd, bf16[640,4096]{1,0:T(8,128)(2,1)} %bitcast.21, bf16[640,4096]{1,0:T(8,128)(2,1)} %bitcast.22, ...), custom_call_target="tpu_custom_call" | custom-call | tf_op jit(solution)/shard_map/density/pallas_call | solution.py:279
  60.5 21.6 %exchange.1 = (bf16[16,64,128]{2,1,0:T(8,128)(2,1)}, bf16[16,64,128]{2,1,0:T(8,128)(2,1)}, bf16[64,128]{1,0:T(8,128)(2,1)}) custom-call(bf16[16,64,128]{2,1,0:T(8,128)(2,1)} %get-tuple-element.10.part, f32[64,128]{1,0:T(8,128)} %bitcast.24, bf16[64,64]{1,0:T(8,128)(2,1)} %constant.150.row, bf16[64,64]{1,0:T(8,128)(2,1)} %constant.151.rowt, ...), custom_call_target="tpu_custom_call" | custom-call | tf_op jit(solution)/shard_map/exchange/pallas_call | solution.py:322
  82.1 0.0 copy-start
  82.1 33.1 %apply.1 = bf16[640,4096]{1,0:T(8,128)(2,1)} custom-call(s32[160]{0:T(256)} %add_clamp_fusion.slots, bf16[160,128,256]{2,1,0:T(8,128)(2,1)} %get-tuple-element.8.fe, bf16[160,128,256]{2,1,0:T(8,128)(2,1)} %get-tuple-element.9.fo, bf16[16,64,128]{2,1,0:T(8,128)(2,1)} %get-tuple-element.11.ve, bf16[16,64,128]{2,1,0:T(8,128)(2,1)} %get-tuple-element.12.vo, ...), custom_call_target="tpu_custom_call" | custom-call | tf_op jit(solution)/shard_map/apply/pallas_call | solution.py:341
  115.2 0.0 copy-done
  115.2 0.6 copy.27
  (4 shorter events, 0.1 us)
Async XLA Ops:
  82.1 33.1 %copy-start = (bf16[64,128]{1,0:T(8,128)(2,1)S(1)}, bf16[64,128]{1,0:T(8,128)(2,1)}, u32[]{:S(2)}) copy-start(bf16[64,128]{1,0:T(8,128)(2,1)} %get-tuple-element.13) | copy-start | bytes 49156

commit v2 on v1

--- a/solution.py
+++ b/solution.py
@@ -39,6 +39,12 @@
     col_pick = np.zeros((2 * coarse, 2 * coarse))
     col_pick[cols, np.arange(2 * coarse)] = 1.0
 
+    tile = 16
+    turn = np.zeros((tile * tile, tile * tile))
+    for r in range(tile):
+        for jj in range(tile):
+            turn[r * tile + jj, jj * tile + r] = 1.0
+
     def low(array):
         return jnp.asarray(np.ascontiguousarray(array), F32).astype(BF16)
 
@@ -47,6 +53,7 @@
         "axt": low(along_x.T),
         "yup": low(np.kron(quad, odd.T)),
         "ydown": low(np.kron(quad, odd)),
+        "turn": low(turn),
         "row": low(row_pick),
         "rowt": low(row_pick.T),
         "col": low(col_pick),
@@ -58,8 +65,15 @@
     return jnp.dot(a, b, preferred_element_type=F32)
 
 
+def stacked(src, r0, lanes):
+    tiles = [src[pl.ds(r0, 16), j * lanes : (j + 1) * lanes] for j in range(32)]
+    return jnp.concatenate(
+        [jnp.concatenate(tiles[:16], axis=0), jnp.concatenate(tiles[16:], axis=0)], axis=1
+    )
+
+
 def density_kernel(
-    coarse, steps, slots, bd, func, resp, ax, yup, fe, fo, part, rm, sf, sr, me, mo, acc
+    coarse, steps, slots, bd, func, resp, ax, yup, turn, fe, fo, part, rm, me, mo, acc
 ):
     step = pl.program_id(0)
     half = coarse // 2
@@ -74,18 +88,18 @@
 
     width = 512
     for c in range(0, coarse * coarse, width):
-        rm[:, c : c + width] = dot(bd[...], resp[:, c : c + width])
+        rm[:, c : c + width] = dot(bd[...], resp[:, c : c + width]).astype(BF16)
 
     def pair(i, carry):
         r0 = pl.multiple_of(i * 16, 16)
         g0 = i * 4
-        for src, s, even, odd, at in ((func, sf, fe, fo, g0), (rm, sr, me, mo, 0)):
-            for j in range(half):
-                s[pl.ds(j, 16, stride=half), :] = src[
-                    pl.ds(r0, 16), j * lanes : (j + 1) * lanes
-                ].astype(F32)
+        for src, even, odd, at in ((func, fe, fo, g0), (rm, me, mo, 0)):
+            t_all = dot(turn[...], stacked(src, r0, lanes))
             for g in range(4):
-                t = [s[(4 * g + k) * half : (4 * g + k + 1) * half, :] for k in range(4)]
+                t = []
+                for k in range(4 * g, 4 * g + 4):
+                    piece = t_all[16 * k : 16 * k + 16]
+                    t.append(jnp.concatenate([piece[:, :lanes], piece[:, lanes:]], axis=0))
                 evens, odds = [], []
                 for k in (0, 2):
                     evens.append(jnp.where(left, t[k], pltpu.roll(t[k + 1], coarse, 1)))
@@ -103,7 +117,7 @@
             for left_src, right_src in ((fe, me), (fo, mo)):
                 total = None
                 for g in (2 * b, 2 * b + 1):
-                    prod = left_src[g0 + g].astype(F32) * right_src[g].astype(F32)
+                    prod = (left_src[g0 + g] * right_src[g]).astype(F32)
                     prod = prod[:, :lanes] + prod[:, lanes:]
                     total = prod if total is None else total + prod
                 sums.append(total + pltpu.roll(total, coarse, 1))
@@ -191,7 +205,7 @@
         second[k].wait_send()
 
 
-def apply_kernel(coarse, slots, fe, fo, ve, vo, axt, ydown, out, s):
+def apply_kernel(coarse, slots, fe, fo, ve, vo, axt, ydown, back, out):
     step = pl.program_id(0)
     half = coarse // 2
     quarter = coarse // 4
@@ -201,6 +215,7 @@
     def pair(i, carry):
         r0 = pl.multiple_of(i * 16, 16)
         g0 = i * 4
+        pieces_out = []
         for b in range(2):
             at = (step * STEP_BOXES + 2 * i + b) * 2
             pieces = []
@@ -220,15 +235,16 @@
                 for k in (0, 2):
                     e = res[:half, k * coarse : (k + 2) * coarse]
                     o = res[half:, k * coarse : (k + 2) * coarse]
-                    base = (4 * g + k) * half
-                    s[base : base + half, :] = jnp.where(left, e, pltpu.roll(o, coarse, 1))
-                    s[base + half : base + 2 * half, :] = jnp.where(
-                        left, pltpu.roll(e, coarse, 1), o
-                    )
+                    first = jnp.where(left, e, pltpu.roll(o, coarse, 1)).astype(BF16)
+                    second = jnp.where(left, pltpu.roll(e, coarse, 1), o).astype(BF16)
+                    for block in (first, second):
+                        pieces_out.append(jnp.concatenate([block[:16], block[16:]], axis=1))
+        flat = dot(back[...], jnp.concatenate(pieces_out, axis=0)).astype(BF16)
         for j in range(half):
-            out[pl.ds(r0, 16), j * lanes : (j + 1) * lanes] = s[
-                pl.ds(j, 16, stride=half), :
-            ].astype(BF16)
+            jj, h = j % 16, j // 16
+            out[pl.ds(r0, 16), j * lanes : (j + 1) * lanes] = flat[
+                16 * jj : 16 * jj + 16, h * lanes : (h + 1) * lanes
+            ]
         return carry
 
     lax.fori_loop(0, STEP_BOXES // 2, pair, 0)
@@ -287,6 +303,7 @@
                 pl.BlockSpec((rows, cells), lambda i, *_: (i, 0)),
                 whole((coarse, coarse)),
                 whole((4 * coarse, 4 * coarse)),
+                whole((256, 256)),
             ],
             out_specs=[
                 pl.BlockSpec((groups, lanes, 4 * coarse), lambda i, *_: (i, 0, 0)),
@@ -294,9 +311,7 @@
                 whole((count, coarse, lanes)),
             ],
             scratch_shapes=[
-                pltpu.VMEM((rows, cells), F32),
-                pltpu.VMEM((16 * coarse // 2, lanes), F32),
-                pltpu.VMEM((16 * coarse // 2, lanes), F32),
+                pltpu.VMEM((rows, cells), BF16),
                 pltpu.VMEM((4, lanes, 4 * coarse), BF16),
                 pltpu.VMEM((4, lanes, 4 * coarse), BF16),
                 pltpu.VMEM((count, coarse, lanes), F32),
@@ -315,6 +330,7 @@
         responses.reshape(boxes * funs, cells),
         t["ax"],
         t["yup"],
+        t["turn"],
     )
 
     vm = pl.BlockSpec(memory_space=pltpu.VMEM)
@@ -350,13 +366,13 @@
                 whole(block),
                 whole((coarse, coarse)),
                 whole((4 * coarse, 4 * coarse)),
+                whole((256, 256)),
             ],
             out_specs=pl.BlockSpec((rows, cells), lambda i, *_: (i, 0)),
-            scratch_shapes=[pltpu.VMEM((16 * coarse // 2, lanes), F32)],
         ),
         out_shape=jax.ShapeDtypeStruct((boxes * funs, cells), BF16),
         name="apply",
-    )(slots, fe, fo, ve, vo, t["axt"], t["ydown"])
+    )(slots, fe, fo, ve, vo, t["axt"], t["ydown"], t["turn"])
     return applied.reshape(boxes, funs, cells), potential.reshape(1, coarse * lanes)
 
 

time: 116 us -> 126 us (1.086)
  Pallas kernels: 107 us -> 117 us
    pallas_call x1, Pallas kernels: 52.2 us -> 58.5 us  [on_device(): pl.pallas_call(functools.partial(density_kernel, coarse, steps), grid_spe...]
    pallas_call x1, Pallas kernels: 33.1 us -> 36.8 us  [on_device(): pl.pallas_call(functools.partial(apply_kernel, coarse), grid_spec=pltpu.P...]
where the time goes in v2:
time: 126 us
  Pallas kernels  117 us (93%)
  other arithmetic  5.28 us (4%)
  local copies, waits for them, and re-layouts  2.92 us (2%)
    pallas_call x1, Pallas kernels, on_device(): pl.pallas_call(functools.partial(density_kernel, coarse, steps), grid_spe...  58.5 us
    pallas_call x1, Pallas kernels, on_device(): pl.pallas_call(functools.partial(apply_kernel, coarse), grid_spec=pltpu.P...  36.8 us
    pallas_call x1, Pallas kernels, on_device(): pl.pallas_call(functools.partial(exchange_kernel, sizes, shifts, own), in...  21.6 us
    reduce_sum x1, other arithmetic, on_device(): mixed = jnp.sum(jnp.where(same, weight_f[..., None], 0.0), axis=2)  2.76 us

profile of v2, /device:TPU:0, one launch (start us, length us, event | category | flops | bytes accessed | tf_op | source)
XLA Modules:
  0.0 125.8 jit_solution(1178002142023349054)
XLA Ops:
  0.7 0.7 fusion.14
  1.4 0.1 broadcast_compare_fusion.1
  1.4 0.7 slice_bitcast_fusion.1
  2.2 0.1 copy.23
  2.3 0.1 subtract_add_fusion
  2.3 0.1 add.119
  2.5 0.1 copy.24
  2.6 0.1 add.125
  2.6 0.1 add.126
  2.8 0.1 add.132
  2.9 0.1 add.133
  3.0 0.6 add_clamp_fusion.slots
  3.6 0.8 copy.25
  4.4 0.3 broadcast_compare_fusion
  4.8 2.8 %select_reduce_fusion = bf16[80,8,128]{2,1,0:T(8,128)(2,1)S(1)} fusion(f32[80,8,24]{2,1,0:T(8,128)S(1)} %fusion, pred[80,24,128]{2,1,0:T(8,128)(4,1)S(1)} %broadcast_compare_fusion), kind=kLoop, calls=%fused_computation | loop fusion | flops 3850240 | bytes 471040 | tf_op jit(solution)/shard_map/reduce_sum | solution.py:285
  7.5 0.7 fusion.1.bd
  8.3 58.5 %density.1 = (bf16[160,128,256]{2,1,0:T(8,128)(2,1)}, bf16[160,128,256]{2,1,0:T(8,128)(2,1)}, bf16[16,64,128]{2,1,0:T(8,128)(2,1)}) custom-call(s32[160]{0:T(256)} %add_clamp_fusion.slots, bf16[640,128]{1,0:T(8,128)(2,1)} %fusion.1.bd, bf16[640,4096]{1,0:T(8,128)(2,1)} %bitcast.21, bf16[640,4096]{1,0:T(8,128)(2,1)} %bitcast.22, ...), custom_call_target="tpu_custom_call" | custom-call | tf_op jit(solution)/shard_map/density/pallas_call | solution.py:295
  66.7 21.6 %exchange.1 = (bf16[16,64,128]{2,1,0:T(8,128)(2,1)}, bf16[16,64,128]{2,1,0:T(8,128)(2,1)}, bf16[64,128]{1,0:T(8,128)(2,1)}) custom-call(bf16[16,64,128]{2,1,0:T(8,128)(2,1)} %get-tuple-element.10.part, f32[64,128]{1,0:T(8,128)} %bitcast.24, bf16[64,64]{1,0:T(8,128)(2,1)} %constant.154.row, bf16[64,64]{1,0:T(8,128)(2,1)} %constant.155.rowt, ...), custom_call_target="tpu_custom_call" | custom-call | tf_op jit(solution)/shard_map/exchange/pallas_call | solution.py:338
  88.3 0.0 copy-start
  88.3 36.8 %apply.1 = bf16[640,4096]{1,0:T(8,128)(2,1)} custom-call(s32[160]{0:T(256)} %add_clamp_fusion.slots, bf16[160,128,256]{2,1,0:T(8,128)(2,1)} %get-tuple-element.8.fe, bf16[160,128,256]{2,1,0:T(8,128)(2,1)} %get-tuple-element.9.fo, bf16[16,64,128]{2,1,0:T(8,128)(2,1)} %get-tuple-element.11.ve, bf16[16,64,128]{2,1,0:T(8,128)(2,1)} %get-tuple-element.12.vo, ...), custom_call_target="tpu_custom_call" | custom-call | tf_op jit(solution)/shard_map/apply/pallas_call | solution.py:357
  125.1 0.0 copy-done
  125.1 0.6 copy.28
  (4 shorter events, 0.1 us)
Async XLA Ops:
  88.3 36.8 %copy-start = (bf16[64,128]{1,0:T(8,128)(2,1)S(1)}, bf16[64,128]{1,0:T(8,128)(2,1)}, u32[]{:S(2)}) copy-start(bf16[64,128]{1,0:T(8,128)(2,1)} %get-tuple-element.13) | copy-start | bytes 49156

commit v3 on v2

--- a/solution.py
+++ b/solution.py
@@ -131,7 +131,7 @@
                     ]
         return carry
 
-    lax.fori_loop(0, STEP_BOXES // 2, pair, 0)
+    lax.fori_loop(0, STEP_BOXES // 2, pair, 0, unroll=8)
 
     @pl.when(step == steps - 1)
     def _():
@@ -205,7 +205,7 @@
         second[k].wait_send()
 
 
-def apply_kernel(coarse, slots, fe, fo, ve, vo, axt, ydown, back, out):
+def apply_kernel(coarse, slots, fe, fo, ve, vo, axt, ydown, out, s):
     step = pl.program_id(0)
     half = coarse // 2
     quarter = coarse // 4
@@ -215,7 +215,6 @@
     def pair(i, carry):
         r0 = pl.multiple_of(i * 16, 16)
         g0 = i * 4
-        pieces_out = []
         for b in range(2):
             at = (step * STEP_BOXES + 2 * i + b) * 2
             pieces = []
@@ -235,19 +234,18 @@
                 for k in (0, 2):
                     e = res[:half, k * coarse : (k + 2) * coarse]
                     o = res[half:, k * coarse : (k + 2) * coarse]
-                    first = jnp.where(left, e, pltpu.roll(o, coarse, 1)).astype(BF16)
-                    second = jnp.where(left, pltpu.roll(e, coarse, 1), o).astype(BF16)
-                    for block in (first, second):
-                        pieces_out.append(jnp.concatenate([block[:16], block[16:]], axis=1))
-        flat = dot(back[...], jnp.concatenate(pieces_out, axis=0)).astype(BF16)
+                    base = (4 * g + k) * half
+                    s[base : base + half, :] = jnp.where(left, e, pltpu.roll(o, coarse, 1))
+                    s[base + half : base + 2 * half, :] = jnp.where(
+                        left, pltpu.roll(e, coarse, 1), o
+                    )
         for j in range(half):
-            jj, h = j % 16, j // 16
-            out[pl.ds(r0, 16), j * lanes : (j + 1) * lanes] = flat[
-                16 * jj : 16 * jj + 16, h * lanes : (h + 1) * lanes
-            ]
+            out[pl.ds(r0, 16), j * lanes : (j + 1) * lanes] = s[
+                pl.ds(j, 16, stride=half), :
+            ].astype(BF16)
         return carry
 
-    lax.fori_loop(0, STEP_BOXES // 2, pair, 0)
+    lax.fori_loop(0, STEP_BOXES // 2, pair, 0, unroll=8)
 
 
 def on_device(sizes, functions, responses, box_domain, pair_index, pair_weight, kernel_xc):
@@ -366,13 +364,13 @@
                 whole(block),
                 whole((coarse, coarse)),
                 whole((4 * coarse, 4 * coarse)),
-                whole((256, 256)),
             ],
             out_specs=pl.BlockSpec((rows, cells), lambda i, *_: (i, 0)),
+            scratch_shapes=[pltpu.VMEM((16 * coarse // 2, lanes), F32)],
         ),
         out_shape=jax.ShapeDtypeStruct((boxes * funs, cells), BF16),
         name="apply",
-    )(slots, fe, fo, ve, vo, t["axt"], t["ydown"], t["turn"])
+    )(slots, fe, fo, ve, vo, t["axt"], t["ydown"])
     return applied.reshape(boxes, funs, cells), potential.reshape(1, coarse * lanes)
 
 

time: 126 us -> 98 us (0.78)
  Pallas kernels: 117 us -> 88.7 us
    pallas_call x1, Pallas kernels: 58.5 us -> 41.6 us  [on_device(): pl.pallas_call(functools.partial(density_kernel, coarse, steps), grid_spe...]
    pallas_call x1, Pallas kernels: 36.8 us -> 25.5 us  [on_device(): pl.pallas_call(functools.partial(apply_kernel, coarse), grid_spec=pltpu.P...]
where the time goes in v3:
time: 98 us; the launch traced here: 97.6 us
  Pallas kernels  88.7 us (91%)
  other arithmetic  5.28 us (5%)
  local copies, waits for them, and re-layouts  2.92 us (3%)
    pallas_call x1, Pallas kernels, on_device(): pl.pallas_call(functools.partial(density_kernel, coarse, steps), grid_spe...  41.6 us
    pallas_call x1, Pallas kernels, on_device(): pl.pallas_call(functools.partial(apply_kernel, coarse), grid_spec=pltpu.P...  25.5 us
    pallas_call x1, Pallas kernels, on_device(): pl.pallas_call(functools.partial(exchange_kernel, sizes, shifts, own), in...  21.6 us
    reduce_sum x1, other arithmetic, on_device(): mixed = jnp.sum(jnp.where(same, weight_f[..., None], 0.0), axis=2)  2.76 us

profile of v3, /device:TPU:0, one launch (start us, length us, event | category | flops | bytes accessed | tf_op | source)
XLA Modules:
  0.0 97.6 jit_solution(8996723425328953352)
XLA Ops:
  0.7 0.7 fusion.14
  1.4 0.1 broadcast_compare_fusion.1
  1.4 0.7 slice_bitcast_fusion.1
  2.2 0.1 copy.23
  2.3 0.1 subtract_add_fusion
  2.3 0.1 add.119
  2.5 0.1 copy.24
  2.6 0.1 add.125
  2.6 0.1 add.126
  2.8 0.1 add.132
  2.9 0.1 add.133
  3.0 0.6 add_clamp_fusion.slots
  3.6 0.8 copy.25
  4.4 0.3 broadcast_compare_fusion
  4.8 2.8 %select_reduce_fusion = bf16[80,8,128]{2,1,0:T(8,128)(2,1)S(1)} fusion(f32[80,8,24]{2,1,0:T(8,128)S(1)} %fusion, pred[80,24,128]{2,1,0:T(8,128)(4,1)S(1)} %broadcast_compare_fusion), kind=kLoop, calls=%fused_computation | loop fusion | flops 3850240 | bytes 471040 | tf_op jit(solution)/shard_map/reduce_sum | solution.py:283
  7.5 0.7 fusion.1.bd
  8.3 41.6 %density.1 = (bf16[160,128,256]{2,1,0:T(8,128)(2,1)}, bf16[160,128,256]{2,1,0:T(8,128)(2,1)}, bf16[16,64,128]{2,1,0:T(8,128)(2,1)}) custom-call(s32[160]{0:T(256)} %add_clamp_fusion.slots, bf16[640,128]{1,0:T(8,128)(2,1)} %fusion.1.bd, bf16[640,4096]{1,0:T(8,128)(2,1)} %bitcast.21, bf16[640,4096]{1,0:T(8,128)(2,1)} %bitcast.22, ...), custom_call_target="tpu_custom_call" | custom-call | tf_op jit(solution)/shard_map/density/pallas_call | solution.py:293
  49.8 21.6 %exchange.1 = (bf16[16,64,128]{2,1,0:T(8,128)(2,1)}, bf16[16,64,128]{2,1,0:T(8,128)(2,1)}, bf16[64,128]{1,0:T(8,128)(2,1)}) custom-call(bf16[16,64,128]{2,1,0:T(8,128)(2,1)} %get-tuple-element.10.part, f32[64,128]{1,0:T(8,128)} %bitcast.24, bf16[64,64]{1,0:T(8,128)(2,1)} %constant.154.row, bf16[64,64]{1,0:T(8,128)(2,1)} %constant.155.rowt, ...), custom_call_target="tpu_custom_call" | custom-call | tf_op jit(solution)/shard_map/exchange/pallas_call | solution.py:336
  71.4 0.0 copy-start
  71.4 25.5 %apply.1 = bf16[640,4096]{1,0:T(8,128)(2,1)} custom-call(s32[160]{0:T(256)} %add_clamp_fusion.slots, bf16[160,128,256]{2,1,0:T(8,128)(2,1)} %get-tuple-element.8.fe, bf16[160,128,256]{2,1,0:T(8,128)(2,1)} %get-tuple-element.9.fo, bf16[16,64,128]{2,1,0:T(8,128)(2,1)} %get-tuple-element.11.ve, bf16[16,64,128]{2,1,0:T(8,128)(2,1)} %get-tuple-element.12.vo, ...), custom_call_target="tpu_custom_call" | custom-call | tf_op jit(solution)/shard_map/apply/pallas_call | solution.py:355
  97.0 0.0 copy-done
  97.0 0.6 copy.28
  (4 shorter events, 0.1 us)
Async XLA Ops:
  71.4 25.6 %copy-start = (bf16[64,128]{1,0:T(8,128)(2,1)S(1)}, bf16[64,128]{1,0:T(8,128)(2,1)}, u32[]{:S(2)}) copy-start(bf16[64,128]{1,0:T(8,128)(2,1)} %get-tuple-element.13) | copy-start | bytes 49156

commit v4 on v3

--- a/solution.py
+++ b/solution.py
@@ -191,7 +191,7 @@
     left = lax.broadcasted_iota(jnp.int32, value.shape, 1) < coarse
 
     def spread(k, block):
-        block = block.astype(F32)
+        block = block.astype(F32) * 0.25
         turned = pltpu.roll(block, coarse, 1)
         ve[k] = jnp.where(left, block, turned).astype(BF16)
         vo[k] = jnp.where(left, turned, block).astype(BF16)
@@ -230,7 +230,7 @@
                 wo = fo[g0 + g] * pieces[1]
                 z = we.astype(F32) + dot(wo, ydown[...])
                 down = dot(axt[...], z[coarse:].astype(BF16))
-                res = (z[:coarse] + down) * 0.25
+                res = z[:coarse] + down
                 for k in (0, 2):
                     e = res[:half, k * coarse : (k + 2) * coarse]
                     o = res[half:, k * coarse : (k + 2) * coarse]

time: 98 us -> 97.9 us (level)
  no operation moved by 1% of the time
where the time goes in v4:
time: 97.9 us; the launch traced here: 97.6 us
  Pallas kernels  88.6 us (91%)
  other arithmetic  5.28 us (5%)
  local copies, waits for them, and re-layouts  2.92 us (3%)
    pallas_call x1, Pallas kernels, on_device(): pl.pallas_call(functools.partial(density_kernel, coarse, steps), grid_spe...  41.6 us
    pallas_call x1, Pallas kernels, on_device(): pl.pallas_call(functools.partial(apply_kernel, coarse), grid_spec=pltpu.P...  25.5 us
    pallas_call x1, Pallas kernels, on_device(): pl.pallas_call(functools.partial(exchange_kernel, sizes, shifts, own), in...  21.6 us
    reduce_sum x1, other arithmetic, on_device(): mixed = jnp.sum(jnp.where(same, weight_f[..., None], 0.0), axis=2)  2.76 us

profile of v4, /device:TPU:0, one launch (start us, length us, event | category | flops | bytes accessed | tf_op | source)
XLA Modules:
  0.0 97.6 jit_solution(1187580473744539484)
XLA Ops:
  0.7 0.7 fusion.14
  1.4 0.1 broadcast_compare_fusion.1
  1.4 0.7 slice_bitcast_fusion.1
  2.2 0.1 copy.23
  2.3 0.1 subtract_add_fusion
  2.3 0.1 add.119
  2.5 0.1 copy.24
  2.6 0.1 add.125
  2.6 0.1 add.126
  2.8 0.1 add.132
  2.9 0.1 add.133
  3.0 0.6 add_clamp_fusion.slots
  3.6 0.8 copy.25
  4.4 0.3 broadcast_compare_fusion
  4.8 2.8 %select_reduce_fusion = bf16[80,8,128]{2,1,0:T(8,128)(2,1)S(1)} fusion(f32[80,8,24]{2,1,0:T(8,128)S(1)} %fusion, pred[80,24,128]{2,1,0:T(8,128)(4,1)S(1)} %broadcast_compare_fusion), kind=kLoop, calls=%fused_computation | loop fusion | flops 3850240 | bytes 471040 | tf_op jit(solution)/shard_map/reduce_sum | solution.py:283
  7.5 0.7 fusion.1.bd
  8.3 41.6 %density.1 = (bf16[160,128,256]{2,1,0:T(8,128)(2,1)}, bf16[160,128,256]{2,1,0:T(8,128)(2,1)}, bf16[16,64,128]{2,1,0:T(8,128)(2,1)}) custom-call(s32[160]{0:T(256)} %add_clamp_fusion.slots, bf16[640,128]{1,0:T(8,128)(2,1)} %fusion.1.bd, bf16[640,4096]{1,0:T(8,128)(2,1)} %bitcast.21, bf16[640,4096]{1,0:T(8,128)(2,1)} %bitcast.22, ...), custom_call_target="tpu_custom_call" | custom-call | tf_op jit(solution)/shard_map/density/pallas_call | solution.py:293
  49.8 21.6 %exchange.1 = (bf16[16,64,128]{2,1,0:T(8,128)(2,1)}, bf16[16,64,128]{2,1,0:T(8,128)(2,1)}, bf16[64,128]{1,0:T(8,128)(2,1)}) custom-call(bf16[16,64,128]{2,1,0:T(8,128)(2,1)} %get-tuple-element.10.part, f32[64,128]{1,0:T(8,128)} %bitcast.24, bf16[64,64]{1,0:T(8,128)(2,1)} %constant.154.row, bf16[64,64]{1,0:T(8,128)(2,1)} %constant.155.rowt, ...), custom_call_target="tpu_custom_call" | custom-call | tf_op jit(solution)/shard_map/exchange/pallas_call | solution.py:336
  71.4 0.0 copy-start
  71.4 25.5 %apply.1 = bf16[640,4096]{1,0:T(8,128)(2,1)} custom-call(s32[160]{0:T(256)} %add_clamp_fusion.slots, bf16[160,128,256]{2,1,0:T(8,128)(2,1)} %get-tuple-element.8.fe, bf16[160,128,256]{2,1,0:T(8,128)(2,1)} %get-tuple-element.9.fo, bf16[16,64,128]{2,1,0:T(8,128)(2,1)} %get-tuple-element.11.ve, bf16[16,64,128]{2,1,0:T(8,128)(2,1)} %get-tuple-element.12.vo, ...), custom_call_target="tpu_custom_call" | custom-call | tf_op jit(solution)/shard_map/apply/pallas_call | solution.py:355
  96.9 0.0 copy-done
  96.9 0.6 copy.28
  (4 shorter events, 0.1 us)
Async XLA Ops:
  71.4 25.5 %copy-start = (bf16[64,128]{1,0:T(8,128)(2,1)S(1)}, bf16[64,128]{1,0:T(8,128)(2,1)}, u32[]{:S(2)}) copy-start(bf16[64,128]{1,0:T(8,128)(2,1)} %get-tuple-element.13) | copy-start | bytes 49156
